TPU v7x, 32 devices: a whole 2x2x4 slice. The times are simulated.
32 devices in a mesh: heads: 4 (over y, core), seq: 8 (over z, x).
Axes of the slice: x: 2, y: 2, z: 4, core: 2. Of those that a mesh axis runs over, the one named last changes fastest.
Arguments:
- queries: bfloat16 [1024, 64, 576], P('seq', 'heads'), may hold values from -6 to 6
- latents: bfloat16 [8, 128, 576], P('seq', 'heads'), may hold values from -6 to 6
- grad_out: bfloat16 [1024, 64, 512], P('seq', 'heads'), may hold values from -6 to 6
- selected: int32 [8, 4], P('seq'), may hold values from 0 to 7, as said below
Outputs:
- output: bfloat16 [1024, 64, 512], P('seq', 'heads')
- grad_query: bfloat16 [1024, 64, 576], P('seq', 'heads')
- latent_grad: float32 [8, 128, 576], P('seq', 'heads')
Inputs may be any that keep to these rules, and one draw needn't show every extreme that they name: `selected`: row i lists 4 different blocks, none of them held on the same index of seq as block i (blocks i and j share it when i // 1 equals j // 1); how often a block is chosen varies widely between blocks.
All inputs are finite; a program needn't handle non-finite values.
Results may differ from a plain program's by a relative error of at most 0.012.
Values may be sent and summed in bfloat16 or wider, within the bound.
A program may use at most 64 MiB of HBM per device.

v0:
```python
import jax
import jax.numpy as jnp
from jax import lax
from jax.sharding import PartitionSpec as P


def shards(queries, latents, grad_out, selected):
    block_count, row_share, key_width = latents.shape
    token_total, head_count, _ = queries.shape
    value_width = grad_out.shape[2]
    key_blocks = selected.shape[1] + 1
    block_size = token_total // block_count
    score_scale = key_width ** (-0.5)
    slices = lax.all_gather(latents, "seq", axis=0, tiled=True)
    list_blocks = slices.shape[0]
    own_blocks = lax.axis_index("seq") * block_count + jnp.arange(block_count, dtype=jnp.int32)
    block_ids = jnp.concatenate([own_blocks[:, None], selected], axis=1).reshape(-1)
    picked = jnp.take(slices, block_ids, axis=0)
    key_row_tiles = lax.all_gather(picked, "heads", axis=1, tiled=True)
    key_row_tiles = key_row_tiles.reshape(block_count, key_blocks * block_size, key_width)
    value_rows = key_row_tiles[:, :, :value_width]
    query_row_tiles = queries.reshape(block_count, block_size, head_count, key_width)
    grad_rows = grad_out.reshape(block_count, block_size, head_count, value_width)
    scores = (
        jnp.einsum(
            "gonv,gmv->gnom", query_row_tiles, key_row_tiles, preferred_element_type=jnp.float32
        )
        * score_scale
    )
    prob_full = jax.nn.softmax(scores, axis=-1)
    prob_half = prob_full.astype(jnp.bfloat16)
    output = jnp.einsum(
        "bhtk,bkl->bthl", prob_half, value_rows, preferred_element_type=jnp.float32
    ).astype(jnp.bfloat16)
    row_delta = jnp.sum(grad_rows.astype(jnp.float32) * output.astype(jnp.float32), axis=-1)
    grad_prob = jnp.einsum(
        "bthl,bkl->bhtk", grad_rows, value_rows, preferred_element_type=jnp.float32
    )
    score_gradient = (
        prob_full * (grad_prob - jnp.transpose(row_delta, (0, 2, 1))[..., None]) * score_scale
    ).astype(jnp.bfloat16)
    grad_query = jnp.einsum(
        "mfgv,mvq->mgfq", score_gradient, key_row_tiles, preferred_element_type=jnp.float32
    ).astype(jnp.bfloat16)
    key_gradient = jnp.einsum(
        "jxnq,jnxa->jqa", score_gradient, query_row_tiles, preferred_element_type=jnp.float32
    )
    grad_value = jnp.einsum(
        "bhtk,bthl->bkl", prob_half, grad_rows, preferred_element_type=jnp.float32
    )
    key_gradient = jnp.concatenate(
        [key_gradient[:, :, :value_width] + grad_value, key_gradient[:, :, value_width:]], axis=-1
    )
    contrib = key_gradient.reshape(block_count * key_blocks, block_size, key_width)
    head_total = lax.psum(contrib, "heads")
    own_share = lax.dynamic_slice_in_dim(
        head_total, lax.axis_index("heads") * row_share, row_share, 1
    )
    one_hot = (jnp.arange(list_blocks, dtype=jnp.int32)[:, None] == block_ids[None, :]).astype(
        jnp.float32
    )
    dense_grad = jnp.dot(
        one_hot,
        own_share.reshape(block_count * key_blocks, row_share * key_width),
        precision=lax.Precision.HIGHEST,
        preferred_element_type=jnp.float32,
    )
    dense_grad = dense_grad.reshape(list_blocks, row_share, key_width)
    holders = list_blocks // block_count
    bundles = dense_grad.reshape(1, holders * block_count, row_share, key_width)
    arrived = lax.all_to_all(bundles, "seq", split_axis=1, concat_axis=0, tiled=True)
    latent_grad = jnp.sum(arrived, axis=0)
    return (
        output.reshape(token_total, head_count, value_width),
        grad_query.reshape(token_total, head_count, key_width),
        latent_grad,
    )


def solution(mesh):
    in_specs = (
        P("seq", "heads", None),
        P("seq", "heads", None),
        P("seq", "heads", None),
        P("seq", None),
    )
    out_specs = (P("seq", "heads", None), P("seq", "heads", None), P("seq", "heads", None))
    return jax.shard_map(shards, mesh=mesh, in_specs=in_specs, out_specs=out_specs, check_vma=False)
```

profile of v0, /device:TPU:0, one launch (start us, length us, event | category | flops | bytes accessed | tf_op | source)
XLA Modules:
  0.0 150.2 jit_solution(12962128840217296627)
XLA Ops:
  7.2 0.0 copy-start
  7.2 0.0 all-reduce.2.cloned.1.call-start
  7.2 0.9 compare_and_fusion
  8.1 32.9 %all_gather.6 = bf16[8,32,576]{2,1,0:T(8,128)(2,1)S(1)} all-gather(bf16[1,32,576]{2,1,0:T(8,128)(2,1)} %param.5), channel_id=1, replica_groups=mesh['heads'=4,'seq'=8] {'seq'}, dimensions={0}, use_global_device_ids=true | all-gather | bytes 331776 | tf_op jit(solution)/shard_map/all_gather | solution.py:14
  41.0 0.6 gather_fusion
  41.6 0.1 broadcast_select_fusion
  41.7 8.8 %all_gather.7 = bf16[5,128,576]{2,1,0:T(8,128)(2,1)S(1)} all-gather(bf16[5,32,576]{2,1,0:T(8,128)(2,1)S(1)} %broadcast_select_fusion), channel_id=1, replica_groups=mesh['heads'=4,'seq'=8] {'heads'}, dimensions={1}, use_global_device_ids=true | all-gather | bytes 921600 | tf_op jit(solution)/shard_map/all_gather | solution.py:19
  50.5 0.0 copy-start.2
  50.5 4.8 %copy.37 = bf16[128,16,512]{0,2,1:T(8,128)(2,1)} copy(bf16[128,16,512]{2,1,0:T(8,128)(2,1)} %param.6) | data formatting | bytes 4194304 | tf_op args[2]
  55.3 0.0 copy-done
  55.3 2.2 %bitcast_reduce_fusion = (f32[16,128]{1,0:T(8,128)S(1)}, f32[640,128,16]{1,0,2:T(8,128)S(1)}) fusion(bf16[640,576,1]{1,0,2:T(8,128)(2,1)S(1)} %bitcast.124, bf16[128,16,576]{0,2,1:T(8,128)(2,1)S(1)} %copy-done), kind=kOutput, calls=%fused_computation.6 | convolution fusion | flops 1512568832 | bytes 8347648 | tf_op jit(solution)/shard_map/gonv,gmv->gnom/dot_general | solution.py:25
  57.5 0.0 copy-start.1
  57.5 0.9 fusion.5
  58.4 0.7 copy-done.1
  59.1 3.5 %fusion.6 = (f32[128,16]{0,1:T(8,128)S(1)}, bf16[512,16,128]{2,0,1:T(8,128)(2,1)}) fusion(bf16[128,16,512]{0,2,1:T(8,128)(2,1)S(1)} %copy-done.1, f32[16,128]{1,0:T(8,128)S(1)} %fusion.5, f32[16,128]{1,0:T(8,128)S(1)} %get-tuple-element.14, f32[640,128,16]{1,0,2:T(8,128)S(1)} %get-tuple-element.15, bf16[1,640,576]{2,1,0:T(8,128)(2,1)S(1)} %bitcast.125), kind=kOutput, calls=%fused_computation.11 | convolution fusion | flops 1352660992 | bytes 10117120 | tf_op jit(solution)/shard_map/bhtk,bkl->bthl/dot_general | solution.py:32
  62.6 0.0 copy-done.2
  62.6 2.0 %fusion.7 = bf16[16,128,640]{1,2,0:T(8,128)(2,1)S(1)} fusion(f32[16,128]{1,0:T(8,128)S(1)} %bitcast.130, f32[16,128]{1,0:T(8,128)S(1)} %fusion.5, f32[16,128]{1,0:T(8,128)S(1)} %get-tuple-element.14, f32[640,128,16]{1,0,2:T(8,128)S(1)} %get-tuple-element.15, bf16[128,16,512]{0,2,1:T(8,128)(2,1)S(1)} %copy-done.1, bf16[1,640,576]{2,1,0:T(8,128)(2,1)S(1)} %bitcast.126), kind=kOutput, calls=%fused_computation.12 | convolution fusion | flops 1351352320 | bytes 10641408 | tf_op jit(solution)/shard_map/bthl,bkl->bhtk/dot_general | solution.py:36
  64.6 0.0 copy-start.3
  64.6 2.0 %convolution_bitcast_fusion = f32[1,640,576]{1,2,0:T(8,128)S(1)} fusion(bf16[16,128,640]{1,2,0:T(8,128)(2,1)S(1)} %fusion.7, bf16[128,16,576]{0,2,1:T(8,128)(2,1)S(1)} %copy-done), kind=kOutput, calls=%fused_computation.21 | convolution fusion | flops 1509949440 | bytes 6455296 | tf_op jit(solution)/shard_map/jxnq,jnxa->jqa/dot_general | solution.py:45
  66.6 0.0 copy-done.3
  66.6 1.9 %fusion.19 = f32[1,640,512]{1,2,0:T(8,128)S(1)} fusion(bf16[128,16,512]{0,2,1:T(8,128)(2,1)S(1)} %copy-done.1, f32[1,640,576]{1,2,0:T(8,128)S(1)} %convolution_bitcast_fusion, f32[16,128]{1,0:T(8,128)S(1)} %fusion.5, f32[16,128]{1,0:T(8,128)S(1)} %get-tuple-element.14, f32[640,128,16]{1,0,2:T(8,128)S(1)} %get-tuple-element.15), kind=kOutput, calls=%fused_computation.23 | convolution fusion | flops 1347747840 | bytes 9977856 | tf_op jit(solution)/shard_map/bhtk,bthl->bkl/dot_general | solution.py:48
  68.6 1.2 pad_maximum_fusion
  69.8 3.0 %copy.43 = f32[1,640,576]{2,1,0:T(8,128)} copy(f32[1,640,576]{1,2,0:T(8,128)} %pad_maximum_fusion) | data formatting | bytes 2949120 | tf_op jit(solution)/shard_map/concatenate | solution.py:51
  72.8 0.0 all-reduce.2.cloned.1.call-update
  72.8 44.1 %all-reduce.2.cloned.1.call-done = f32[5,128,576]{2,1,0:T(8,128)} async-done(((f32[5,128,576]{2,1,0:T(8,128)}), f32[5,128,576]{2,1,0:T(8,128)}) %all-reduce.2.cloned.1.call-update) | async-done | bytes 1474576 | tf_op jit(solution)/shard_map/psum | solution.py:55
  117.0 1.0 constant_dynamic-slice_fusion
  118.0 0.2 reshape.186
  118.2 0.2 dot_general.43
  118.4 0.7 convolution_bitcast_fusion.1
  119.1 1.0 copy.45
  120.0 5.5 %all-to-all-start = ((f32[1,8,32,576]{3,2,0,1:T(8,128)}), f32[1,8,32,576]{3,2,0,1:T(8,128)S(1)}, u32[]{:S(2)}, u32[]{:S(2)}) async-start(f32[1,8,32,576]{3,2,0,1:T(8,128)} %copy.45), calls=%async_computation | async-start | bytes 1310720 | tf_op jit(solution)/shard_map/all_to_all | solution.py:71
  125.5 4.5 %copy.46 = bf16[128,16,512]{2,1,0:T(8,128)(2,1)} copy(bf16[128,16,512]{0,2,1:T(8,128)(2,1)} %bitcast.123) | data formatting | bytes 4194304
  130.1 5.4 %convert_bitcast_fusion = bf16[128,16,576]{0,2,1:T(8,128)(2,1)} fusion(bf16[640,576,1]{1,0,2:T(8,128)(2,1)} %bitcast.127, bf16[16,128,640]{1,2,0:T(8,128)(2,1)} %copy-done.3), kind=kOutput, calls=%fused_computation.18 | convolution fusion | flops 1511129088 | bytes 5718016 | tf_op jit(solution)/shard_map/mfgv,mvq->mgfq/dot_general | solution.py:42
  135.5 7.2 %all-to-all-done = f32[1,8,32,576]{3,2,0,1:T(8,128)S(1)} async-done(((f32[1,8,32,576]{3,2,0,1:T(8,128)}), f32[1,8,32,576]{3,2,0,1:T(8,128)S(1)}, u32[]{:S(2)}, u32[]{:S(2)}) %all-to-all-start) | async-done | bytes 589856 | tf_op jit(solution)/shard_map/all_to_all | solution.py:71
  142.7 0.7 reduce_sum.34
  (3 shorter events, 0.0 us)
Async XLA Ops:
  7.2 48.1 %copy-start = (bf16[128,16,576]{0,2,1:T(8,128)(2,1)S(1)}, bf16[128,16,576]{0,2,1:T(8,128)(2,1)}, u32[]{:S(2)}) copy-start(bf16[128,16,576]{0,2,1:T(8,128)(2,1)} %param.4) | copy-start | bytes 7077892
  7.2 109.8 %all-reduce.2.cloned.1.call-start = ((), (), s32[]{:S(2)}) async-start(), calls=%async_computation.1 | async-start | bytes 3276800 | tf_op jit(solution)/shard_map/psum | solution.py:55
  50.5 12.1 %copy-start.2 = (bf16[5,128,576]{2,1,0:T(8,128)(2,1)}, bf16[5,128,576]{2,1,0:T(8,128)(2,1)S(1)}, u32[]{:S(2)}) copy-start(bf16[5,128,576]{2,1,0:T(8,128)(2,1)S(1)} %all_gather.7) | copy-start | bytes 2211844
  57.5 1.6 %copy-start.1 = (bf16[128,16,512]{0,2,1:T(8,128)(2,1)S(1)}, bf16[128,16,512]{0,2,1:T(8,128)(2,1)}, u32[]{:S(2)}) copy-start(bf16[128,16,512]{0,2,1:T(8,128)(2,1)} %copy.37) | copy-start | bytes 6291460
  64.6 2.0 %copy-start.3 = (bf16[16,128,640]{1,2,0:T(8,128)(2,1)}, bf16[16,128,640]{1,2,0:T(8,128)(2,1)S(1)}, u32[]{:S(2)}) copy-start(bf16[16,128,640]{1,2,0:T(8,128)(2,1)S(1)} %fusion.7) | copy-start | bytes 7864324
  120.0 22.7 %all-to-all-start = ((f32[1,8,32,576]{3,2,0,1:T(8,128)}), f32[1,8,32,576]{3,2,0,1:T(8,128)S(1)}, u32[]{:S(2)}, u32[]{:S(2)}) async-start(f32[1,8,32,576]{3,2,0,1:T(8,128)} %copy.45), calls=%async_computation | async-start | bytes 1310720 | tf_op jit(solution)/shard_map/all_to_all | solution.py:71
Sparse Core Ops, SparseCore 0:
  73.0 43.9 all-reduce.1
where the time goes:
time: 151 us; the launch traced here: 150 us
  waiting for transfers between devices  51.3 us (34%)
  blocking collectives  41.7 us (28%)
  matrix products  17.7 us (12%)
  local copies, waits for them, and re-layouts  16.1 us (11%)
  between operations  14.1 us (9%)
  starting transfers between devices  5.55 us (4%)
  other arithmetic  3.74 us (2%)
    psum x1, waiting for transfers between devices, shards(): head_total = lax.psum(contrib, 'heads')  44.1 us
    all_gather x1, blocking collectives, shards(): slices = lax.all_gather(latents, 'seq', axis=0, tiled=True)  32.9 us
    unnamed x10, local copies, waits for them, and re-layouts  10 us
    all_gather x1, blocking collectives, shards(): key_row_tiles = lax.all_gather(picked, 'heads', axis=1, tiled=True)  8.8 us
    all_to_all x1, waiting for transfers between devices, shards(): lax.all_to_all(bundles, 'seq', split_axis=1, concat_axis=0, tiled=True)  7.21 us
    all_to_all x1, starting transfers between devices, shards(): lax.all_to_all(bundles, 'seq', split_axis=1, concat_axis=0, tiled=True)  5.51 us
    dot_general x1, matrix products, shards(): jnp.einsum('mfgv,mvq->mgfq', score_gradient, key_row_tiles, preferred_ele...  5.43 us
    dot_general x1, matrix products, shards(): jnp.einsum('bhtk,bkl->bthl', prob_half, value_rows, preferred_element_typ...  3.47 us
  transfers between devices with their start and end apart: 2, of which 2 were waited for; matrix products, arithmetic and copies ran while one was open for 7% of the time, Pallas kernels for 0%

commit v1 on v0

v1 whole, which is shorter than its diff:
```python
import functools

import jax
import jax.numpy as jnp
from jax import lax
from jax.experimental import pallas as pl
from jax.experimental.pallas import tpu as pltpu
from jax.sharding import PartitionSpec as P

MESH = pl.DeviceIdType.MESH
VMEM = pltpu.MemorySpace.VMEM
SMEM = pltpu.MemorySpace.SMEM


def place(dims):
    a_n, b_n, g_n, c_n = dims
    s, h = lax.axis_index("seq"), lax.axis_index("heads")
    return s // b_n, lax.rem(s, b_n), h // c_n, lax.rem(h, c_n)


def other(x, k, n):
    return lax.rem(x + k, n)


def greet(dims, me):
    a_n, b_n, g_n, c_n = dims
    a, b, g, c = me
    barrier = pltpu.get_barrier_semaphore()

    def signal(a2, b2, g2, c2):
        pl.semaphore_signal(
            barrier, inc=1, device_id=(g2 * c_n + c2, a2 * b_n + b2), device_id_type=MESH
        )

    for k in range(1, c_n):
        signal(a, b, g, other(c, k, c_n))
    for k in range(1, b_n):
        signal(a, other(b, k, b_n), g, c)
    for k in range(1, g_n):
        signal(a, b, other(g, k, g_n), c)
    for k in range(1, a_n):
        signal(other(a, k, a_n), b, g, c)
    pl.semaphore_wait(barrier, a_n + b_n + g_n + c_n - 4)


def gather_kernel(dims, own_ref, out_ref, own_sem, a_sem, b_sem, g_sem, c_sem, recv_sem):
    a_n, b_n, g_n, c_n = dims
    me = place(dims)
    a, b, g, c = me
    mine = pltpu.make_async_copy(own_ref.at[0], out_ref.at[a * b_n + b, g * c_n + c], own_sem)
    mine.start()
    greet(dims, me)

    def copy(piece, target, sem, own=False):
        a1, b1, g1, c1 = piece
        a2, b2, g2, c2 = target
        slot = (a1 * b_n + b1, g1 * c_n + c1)
        return pltpu.make_async_remote_copy(
            src_ref=own_ref.at[0] if own else out_ref.at[slot],
            dst_ref=out_ref.at[slot],
            send_sem=sem,
            recv_sem=recv_sem.at[slot],
            device_id=(g2 * c_n + c2, a2 * b_n + b2),
            device_id_type=MESH,
        )

    def to_a(k, own=True):
        return copy(me, (other(a, k, a_n), b, g, c), a_sem.at[k], own)

    def to_b(piece, k, own=False):
        return copy(piece, (a, other(b, k, b_n), g, c), b_sem.at[piece[0], k], own)

    def to_g(piece, k, own=False):
        return copy(
            piece, (a, b, other(g, k, g_n), c), g_sem.at[piece[0] * b_n + piece[1], k], own
        )

    def to_c(piece, k, own=False):
        return copy(
            piece,
            (a, b, g, other(c, k, c_n)),
            c_sem.at[piece[0] * b_n + piece[1], piece[2], k],
            own,
        )

    def arrived(piece):
        copy(piece, (a, b, g, c), own_sem).wait_recv()

    for k in range(1, a_n):
        to_a(k).start()
    for k in range(1, g_n):
        to_g(me, k, True).start()
    for k in range(1, b_n):
        to_b(me, k, True).start()
    for k in range(1, c_n):
        to_c(me, k, True).start()

    def forward(k, first):
        a1 = other(a, k, a_n)
        piece = (a1, b, g, c)
        if not first:
            arrived(piece)
            for n in range(1, g_n):
                to_g(piece, n).start()
            for n in range(1, b_n):
                to_b(piece, n).start()
            for n in range(1, c_n):
                to_c(piece, n).start()
        for n in range(1, b_n):
            piece = (a1, other(b, n, b_n), g, c)
            arrived(piece)
            for m in range(1, g_n):
                to_g(piece, m).start()
            for m in range(1, c_n):
                to_c(piece, m).start()
        for n in range(b_n):
            for m in range(1, g_n):
                piece = (a1, other(b, n, b_n), other(g, m, g_n), c)
                arrived(piece)
                for i in range(1, c_n):
                    to_c(piece, i).start()

    forward(0, True)
    if a_n > 1:
        lax.fori_loop(1, a_n, lambda k, _: (forward(k, False), 0)[1], 0)

    def finish(k, _):
        a1 = other(a, k, a_n)
        for n in range(b_n):
            b1 = other(b, n, b_n)
            for m in range(1, g_n):
                to_g((a1, b1, g, c), m).wait_send()
            for m in range(g_n):
                g1 = other(g, m, g_n)
                for i in range(1, c_n):
                    to_c((a1, b1, g1, c), i).wait_send()
                    arrived((a1, b1, g1, other(c, i, c_n)))
        for n in range(1, b_n):
            to_b((a1, b, g, c), n).wait_send()
        return 0

    lax.fori_loop(0, a_n, finish, 0)
    for k in range(1, a_n):
        to_a(k).wait_send()
    mine.wait()


def gather_latents(latents, dims):
    a_n, b_n, g_n, c_n = dims
    _, row_share, key_width = latents.shape
    n_s, n_h = a_n * b_n, g_n * c_n
    dma = pltpu.SemaphoreType.DMA
    return pl.pallas_call(
        functools.partial(gather_kernel, dims),
        out_shape=jax.ShapeDtypeStruct((n_s, n_h, row_share, key_width), latents.dtype),
        in_specs=[pl.BlockSpec(memory_space=VMEM)],
        out_specs=pl.BlockSpec(memory_space=VMEM),
        scratch_shapes=[
            dma,
            dma((a_n,)),
            dma((a_n, b_n)),
            dma((n_s, g_n)),
            dma((n_s, g_n, c_n)),
            dma((n_s, n_h)),
        ],
        compiler_params=pltpu.CompilerParams(collective_id=0, has_side_effects=True),
        name="gather_latents",
    )(latents)


def attend_kernel(
    scale, value_width, sel_ref, all_ref, q_ref, g_ref, o_ref, dq_ref, con_ref, keys, acc
):
    step = pl.program_id(0)
    block = all_ref.shape[1]
    count = sel_ref.shape[1] + 1

    @pl.when(step == 0)
    def _():
        keys[:block, :] = all_ref[lax.axis_index("seq")]
        for n in range(1, count):
            keys[n * block : (n + 1) * block, :] = all_ref[sel_ref[0, n - 1]]
        acc[...] = jnp.zeros_like(acc)

    f32 = jnp.float32
    q, g = q_ref[...], g_ref[...]
    across = (((1,), (1,)), ((), ()))
    down = (((0,), (0,)), ((), ()))
    scores = lax.dot_general(q, keys[...], across, preferred_element_type=f32)
    top = jnp.max(scores, axis=-1, keepdims=True)
    weights = jnp.exp((scores - top) * scale)
    probs = weights * (1.0 / jnp.sum(weights, axis=-1, keepdims=True))
    half = probs.astype(jnp.bfloat16)
    values = keys[:, :value_width]
    out = jnp.dot(half, values, preferred_element_type=f32).astype(jnp.bfloat16)
    o_ref[...] = out
    delta = jnp.sum(g.astype(f32) * out.astype(f32), axis=-1, keepdims=True)
    grad_prob = lax.dot_general(g, values, across, preferred_element_type=f32)
    grad_score = (probs * (grad_prob - delta) * scale).astype(jnp.bfloat16)
    dq_ref[...] = jnp.dot(grad_score, keys[...], preferred_element_type=f32).astype(jnp.bfloat16)
    acc[...] += lax.dot_general(grad_score, q, down, preferred_element_type=f32)
    acc[:, :value_width] += lax.dot_general(half, g, down, preferred_element_type=f32)

    @pl.when(step == pl.num_programs(0) - 1)
    def _():
        con_ref[...] = acc[...].astype(jnp.bfloat16)


def attend(selected, all_keys, queries, grad_out):
    rows, key_width = queries.shape
    value_width = grad_out.shape[1]
    keys = (selected.shape[1] + 1) * all_keys.shape[1]
    tile = min(rows, 256)
    return pl.pallas_call(
        functools.partial(attend_kernel, key_width ** (-0.5), value_width),
        grid=(rows // tile,),
        out_shape=(
            jax.ShapeDtypeStruct((rows, value_width), jnp.bfloat16),
            jax.ShapeDtypeStruct((rows, key_width), jnp.bfloat16),
            jax.ShapeDtypeStruct((keys, key_width), jnp.bfloat16),
        ),
        in_specs=[
            pl.BlockSpec(memory_space=SMEM),
            pl.BlockSpec(all_keys.shape, lambda i: (0, 0, 0)),
            pl.BlockSpec((tile, key_width), lambda i: (i, 0)),
            pl.BlockSpec((tile, value_width), lambda i: (i, 0)),
        ],
        out_specs=(
            pl.BlockSpec((tile, value_width), lambda i: (i, 0)),
            pl.BlockSpec((tile, key_width), lambda i: (i, 0)),
            pl.BlockSpec((keys, key_width), lambda i: (0, 0)),
        ),
        scratch_shapes=[
            pltpu.VMEM((keys, key_width), jnp.bfloat16),
            pltpu.VMEM((keys, key_width), jnp.float32),
        ],
        name="attend",
    )(selected, all_keys, queries, grad_out)


def reduce_kernel(
    dims, sel_ref, con_ref, out_ref,
    c_in, g_out, g_in, sums, b_out, b_in, a_out, a_in,
    c_sem, g_sem, b_sem, a_sem,
):
    a_n, b_n, g_n, c_n = dims
    me = place(dims)
    a, b, g, c = me
    count = con_ref.shape[0]
    f32, bf16 = jnp.float32, jnp.bfloat16
    greet(dims, me)

    def copy(src, dst, sems, there):
        a2, b2, g2, c2 = there
        return pltpu.make_async_remote_copy(
            src_ref=src,
            dst_ref=dst,
            send_sem=sems.at[0],
            recv_sem=sems.at[1],
            device_id=(g2 * c_n + c2, a2 * b_n + b2),
            device_id_type=MESH,
        )

    def to_c(p, k):
        c2 = other(c, k, c_n)
        return copy(con_ref.at[p, :, c2], c_in.at[p, k], c_sem.at[p, k], (a, b, g, c2))

    def to_g(p, k):
        return copy(g_out.at[p, k], g_in.at[p, k], g_sem.at[p, k], (a, b, other(g, k, g_n), c))

    def to_b(k, n):
        return copy(b_out.at[k, n], b_in.at[k, n], b_sem.at[k, n], (a, other(b, n, b_n), g, c))

    def to_a(k):
        return copy(a_out.at[k], a_in.at[k], a_sem.at[k], (other(a, k, a_n), b, g, c))

    for p in range(count):
        for k in range(1, c_n):
            to_c(p, k).start()

    def chip_sum(p, g1):
        total = con_ref[p, g1, c].astype(f32)
        for k in range(1, c_n):
            total += c_in[p, k, g1].astype(f32)
        return total

    for p in range(count):
        for k in range(1, c_n):
            to_c(p, k).wait_recv()
        for k in range(1, g_n):
            g_out[p, k] = chip_sum(p, other(g, k, g_n)).astype(bf16)
            to_g(p, k).start()
    sums[count] = jnp.zeros(sums.shape[1:], f32)
    for p in range(count):
        total = chip_sum(p, g)
        for k in range(1, g_n):
            to_g(p, k).wait_recv()
            total += g_in[p, k].astype(f32)
        sums[p] = total

    def dense(a1, b1):
        block = a1 * b_n + b1
        at = jnp.where(block == a * b_n + b, 0, count)
        for n in range(1, count):
            at = jnp.where(sel_ref[0, n - 1] == block, n, at)
        return sums[at]

    def send_b(k, _):
        for n in range(1, b_n):
            b_out[k, n] = dense(other(a, k, a_n), other(b, n, b_n)).astype(bf16)
            to_b(k, n).start()
        return 0

    def send_a(k, _):
        total = dense(other(a, k, a_n), b)
        for n in range(1, b_n):
            to_b(k, n).wait_recv()
            total += b_in[k, n].astype(f32)
        a_out[k] = total.astype(bf16)
        to_a(k).start()
        return 0

    if b_n > 1:
        lax.fori_loop(1, a_n, send_b, 0)
        send_b(0, 0)
    lax.fori_loop(1, a_n, send_a, 0)
    total = dense(a, b)
    for n in range(1, b_n):
        to_b(0, n).wait_recv()
        total += b_in[0, n].astype(f32)
    out_ref[...] = total

    def take_a(k, _):
        to_a(k).wait_recv()
        out_ref[...] += a_in[k].astype(f32)
        return 0

    lax.fori_loop(1, a_n, take_a, 0)

    def finish(k, _):
        to_a(k).wait_send()
        for n in range(1, b_n):
            to_b(k, n).wait_send()
        return 0

    lax.fori_loop(1, a_n, finish, 0)
    for n in range(1, b_n):
        to_b(0, n).wait_send()
    for p in range(count):
        for k in range(1, c_n):
            to_c(p, k).wait_send()
        for k in range(1, g_n):
            to_g(p, k).wait_send()


def reduce_grads(selected, contrib, dims):
    a_n, b_n, g_n, c_n = dims
    count = selected.shape[1] + 1
    keys, key_width = contrib.shape
    rows = keys // count // (g_n * c_n)
    contrib = contrib.reshape(count, g_n, c_n, rows, key_width)
    one = (rows, key_width)
    dma = pltpu.SemaphoreType.DMA
    half = functools.partial(pltpu.VMEM, dtype=jnp.bfloat16)
    return pl.pallas_call(
        functools.partial(reduce_kernel, dims),
        out_shape=jax.ShapeDtypeStruct(one, jnp.float32),
        in_specs=[pl.BlockSpec(memory_space=SMEM), pl.BlockSpec(memory_space=VMEM)],
        out_specs=pl.BlockSpec(memory_space=VMEM),
        scratch_shapes=[
            half((count, c_n, g_n) + one),
            half((count, g_n) + one),
            half((count, g_n) + one),
            pltpu.VMEM((count + 1,) + one, jnp.float32),
            half((a_n, b_n) + one),
            half((a_n, b_n) + one),
            half((a_n,) + one),
            half((a_n,) + one),
            dma((count, c_n, 2)),
            dma((count, g_n, 2)),
            dma((a_n, b_n, 2)),
            dma((a_n, 2)),
        ],
        compiler_params=pltpu.CompilerParams(collective_id=1, has_side_effects=True),
        name="reduce_grads",
    )(selected, contrib)


def shards(dims, queries, latents, grad_out, selected):
    block_count, row_share, key_width = latents.shape
    token_total, head_count, _ = queries.shape
    value_width = grad_out.shape[2]
    assert block_count == 1
    rows = token_total * head_count
    pieces = gather_latents(latents, dims)
    all_keys = pieces.reshape(pieces.shape[0], -1, key_width)
    output, grad_query, contrib = attend(
        selected, all_keys, queries.reshape(rows, key_width), grad_out.reshape(rows, value_width)
    )
    latent_grad = reduce_grads(selected, contrib, dims)
    return (
        output.reshape(token_total, head_count, value_width),
        grad_query.reshape(token_total, head_count, key_width),
        latent_grad[None],
    )


def solution(mesh):
    n_h, n_s = mesh.shape["heads"], mesh.shape["seq"]
    b_n = 2 if n_s % 2 == 0 else 1
    c_n = 2 if n_h % 2 == 0 else 1
    dims = (n_s // b_n, b_n, n_h // c_n, c_n)
    in_specs = (
        P("seq", "heads", None),
        P("seq", "heads", None),
        P("seq", "heads", None),
        P("seq", None),
    )
    out_specs = (P("seq", "heads", None), P("seq", "heads", None), P("seq", "heads", None))
    return jax.shard_map(
        functools.partial(shards, dims),
        mesh=mesh, in_specs=in_specs, out_specs=out_specs, check_vma=False,
    )
```

time: 151 us -> 85.7 us (0.57)
  Pallas kernels: 0 us -> 73.5 us
  waiting for transfers between devices: 51.3 us -> 0 us
  blocking collectives: 41.7 us -> 0 us
  matrix products: 17.7 us -> 0 us
  between operations: 14.1 us -> 0.65 us
  starting transfers between devices: 5.55 us -> 0 us
  local copies, waits for them, and re-layouts: 16.1 us -> 11.1 us
  other arithmetic: 3.74 us -> 0 us
    pallas_call x0 -> x3, Pallas kernels: none -> 73.5 us  [the longest x1 32.7 us: gather_latents(): pl.pallas_call(functools.partial(gather_kernel, dims), out_shape=jax.Shap...]
    psum x1 -> x0, waiting for transfers between devices: 44.1 us -> none  [shards(): head_total = lax.psum(contrib, 'heads')]
    all_gather x2 -> x0, blocking collectives: 41.7 us -> none  [the longest x1 32.9 us: shards(): slices = lax.all_gather(latents, 'seq', axis=0, tiled=True)]
    dot_general x7 -> x0, matrix products: 17.7 us -> none  [the longest x1 5.43 us: shards(): jnp.einsum('mfgv,mvq->mgfq', score_gradient, key_row_tiles, preferred_ele...]
    all_to_all x1 -> x0, waiting for transfers between devices: 7.21 us -> none  [shards(): lax.all_to_all(bundles, 'seq', split_axis=1, concat_axis=0, tiled=True)]
    all_to_all x1 -> x0, starting transfers between devices: 5.51 us -> none  [shards(): lax.all_to_all(bundles, 'seq', split_axis=1, concat_axis=0, tiled=True)]
    concatenate x1 -> x0, local copies, waits for them, and re-layouts: 3.04 us -> none  [shards(): jnp.concatenate([key_gradient[:, :, :value_width] + grad_value, key_gradi...]
    reduce_sum x2 -> x0, other arithmetic: 1.54 us -> none  [the longest x1 0.87 us: shards(): prob_full = jax.nn.softmax(scores, axis=-1)]
  transfers between devices with their start and end apart: 2 -> 0, of which waited for: 2 -> 0; matrix products, arithmetic and copies ran while one was open for 7% -> 0% of each run, Pallas kernels for 0% -> 0%
where the time goes in v1:
time: 85.7 us; the launch traced here: 85.3 us
  Pallas kernels  73.5 us (86%)
  local copies, waits for them, and re-layouts  11.1 us (13%)
    pallas_call x1, Pallas kernels, gather_latents(): pl.pallas_call(functools.partial(gather_kernel, dims), out_shape=jax.Shap...  32.7 us
    pallas_call x1, Pallas kernels, reduce_grads(): pl.pallas_call(functools.partial(reduce_kernel, dims), out_shape=jax.Shap...  21.3 us
    pallas_call x1, Pallas kernels, attend(): pl.pallas_call(functools.partial(attend_kernel, key_width ** (-0.5), valu...  19.6 us
    unnamed x3, local copies, waits for them, and re-layouts  11.1 us

profile of v1, /device:TPU:0, one launch (start us, length us, event | category | flops | bytes accessed | tf_op | source)
XLA Modules:
  0.0 85.3 jit_solution(3439462045907462052)
XLA Ops:
  0.6 32.7 %gather_latents.1 = bf16[8,4,32,576]{3,2,1,0:T(8,128)(2,1)} custom-call(bf16[1,32,576]{2,1,0:T(8,128)(2,1)} %own_ref.1), custom_call_target="tpu_custom_call" | custom-call | tf_op jit(solution)/shard_map/gather_latents/pallas_call | solution.py:153
  33.3 4.9 %copy.7 = bf16[128,16,576]{2,1,0:T(8,128)(2,1)} copy(bf16[128,16,576]{0,2,1:T(8,128)(2,1)} %param.4) | data formatting | bytes 4718592 | tf_op args[0]
  38.2 19.6 %attend.1 = (bf16[2048,512]{1,0:T(8,128)(2,1)}, bf16[2048,576]{1,0:T(8,128)(2,1)}, bf16[640,576]{1,0:T(8,128)(2,1)}) custom-call(s32[1,4]{1,0:T(1,128)} %sel_ref.3, bf16[8,128,576]{2,1,0:T(8,128)(2,1)} %bitcast.8, bf16[2048,576]{1,0:T(8,128)(2,1)} %bitcast.7, bf16[2048,512]{1,0:T(8,128)(2,1)} %bitcast.10), custom_call_target="tpu_custom_call" | custom-call | tf_op jit(solution)/shard_map/attend/pallas_call | solution.py:214
  57.8 4.7 %copy.8 = bf16[128,16,576]{0,2,1:T(8,128)(2,1)} copy(bf16[128,16,576]{2,1,0:T(8,128)(2,1)} %bitcast.9) | data formatting | bytes 4718592
  62.5 21.3 %reduce_grads.1 = f32[32,576]{1,0:T(8,128)} custom-call(s32[1,4]{1,0:T(1,128)} %sel_ref.3, bf16[5,2,2,32,576]{4,3,2,1,0:T(8,128)(2,1)} %bitcast.11), custom_call_target="tpu_custom_call" | custom-call | tf_op jit(solution)/shard_map/reduce_grads/pallas_call | solution.py:365
  83.8 1.5 %copy.10 = f32[1,32,576]{2,1,0:T(8,128)} copy(f32[1,32,576]{2,1,0:T(8,128)} %bitcast.12) | data formatting | bytes 147456

commit v2 on v1

--- a/solution.py
+++ b/solution.py
@@ -51,9 +51,18 @@
     mine.start()
     greet(dims, me)
 
-    def copy(piece, target, sem, own=False):
-        a1, b1, g1, c1 = piece
-        a2, b2, g2, c2 = target
+    swap = b_n == g_n
+    flip = lax.rem(c, 2) if swap else 0
+
+    def spot(ka, kp, kq, kc):
+        kb, kg = (flip * kp + (1 - flip) * kq, (1 - flip) * kp + flip * kq) if swap else (kq, kp)
+        return other(a, ka, a_n), other(b, kb, b_n), other(g, kg, g_n), other(c, kc, c_n)
+
+    p_n, q_n = g_n, b_n
+
+    def copy(key, step, sem, own):
+        a1, b1, g1, c1 = spot(*key)
+        a2, b2, g2, c2 = spot(*step)
         slot = (a1 * b_n + b1, g1 * c_n + c1)
         return pltpu.make_async_remote_copy(
             src_ref=own_ref.at[0] if own else out_ref.at[slot],
@@ -64,84 +73,62 @@
             device_id_type=MESH,
         )
 
-    def to_a(k, own=True):
-        return copy(me, (other(a, k, a_n), b, g, c), a_sem.at[k], own)
-
-    def to_b(piece, k, own=False):
-        return copy(piece, (a, other(b, k, b_n), g, c), b_sem.at[piece[0], k], own)
-
-    def to_g(piece, k, own=False):
-        return copy(
-            piece, (a, b, other(g, k, g_n), c), g_sem.at[piece[0] * b_n + piece[1], k], own
-        )
-
-    def to_c(piece, k, own=False):
-        return copy(
-            piece,
-            (a, b, g, other(c, k, c_n)),
-            c_sem.at[piece[0] * b_n + piece[1], piece[2], k],
-            own,
-        )
-
-    def arrived(piece):
-        copy(piece, (a, b, g, c), own_sem).wait_recv()
-
-    for k in range(1, a_n):
-        to_a(k).start()
-    for k in range(1, g_n):
-        to_g(me, k, True).start()
-    for k in range(1, b_n):
-        to_b(me, k, True).start()
-    for k in range(1, c_n):
-        to_c(me, k, True).start()
-
-    def forward(k, first):
-        a1 = other(a, k, a_n)
-        piece = (a1, b, g, c)
-        if not first:
-            arrived(piece)
-            for n in range(1, g_n):
-                to_g(piece, n).start()
-            for n in range(1, b_n):
-                to_b(piece, n).start()
-            for n in range(1, c_n):
-                to_c(piece, n).start()
-        for n in range(1, b_n):
-            piece = (a1, other(b, n, b_n), g, c)
-            arrived(piece)
-            for m in range(1, g_n):
-                to_g(piece, m).start()
-            for m in range(1, c_n):
-                to_c(piece, m).start()
-        for n in range(b_n):
-            for m in range(1, g_n):
-                piece = (a1, other(b, n, b_n), other(g, m, g_n), c)
-                arrived(piece)
-                for i in range(1, c_n):
-                    to_c(piece, i).start()
-
-    forward(0, True)
-    if a_n > 1:
-        lax.fori_loop(1, a_n, lambda k, _: (forward(k, False), 0)[1], 0)
-
-    def finish(k, _):
-        a1 = other(a, k, a_n)
-        for n in range(b_n):
-            b1 = other(b, n, b_n)
-            for m in range(1, g_n):
-                to_g((a1, b1, g, c), m).wait_send()
-            for m in range(g_n):
-                g1 = other(g, m, g_n)
-                for i in range(1, c_n):
-                    to_c((a1, b1, g1, c), i).wait_send()
-                    arrived((a1, b1, g1, other(c, i, c_n)))
-        for n in range(1, b_n):
-            to_b((a1, b, g, c), n).wait_send()
-        return 0
-
-    lax.fori_loop(0, a_n, finish, 0)
-    for k in range(1, a_n):
-        to_a(k).wait_send()
+    def arrived(*key):
+        copy(key, (0, 0, 0, 0), own_sem, False).wait_recv()
+
+    def sends(ka, kp, kq, own=False):
+        key = (ka, kp, kq, 0)
+        out = []
+        if isinstance(kp, int) and kp == 0 and isinstance(kq, int) and kq == 0:
+            out += [copy(key, (0, n, 0, 0), b_sem.at[ka, n], own) for n in range(1, p_n)]
+        if isinstance(kq, int) and kq == 0:
+            out += [copy(key, (0, 0, n, 0), g_sem.at[ka * p_n + kp, n], own) for n in range(1, q_n)]
+        out += [
+            copy(key, (0, 0, 0, n), c_sem.at[ka * p_n + kp, kq, n], own) for n in range(1, c_n)
+        ]
+        return out
+
+    def firsts():
+        return [copy((0, 0, 0, 0), (n, 0, 0, 0), a_sem.at[n], True) for n in range(1, a_n)]
+
+    def over_a(fn):
+        if a_n <= 8:
+            for ka in range(1, a_n):
+                fn(ka)
+        elif a_n > 1:
+            lax.fori_loop(1, a_n, lambda ka, _: (fn(ka), 0)[1], 0)
+
+    def relay(ka, kp, kq):
+        arrived(ka, kp, kq, 0)
+        for cp in sends(ka, kp, kq):
+            cp.start()
+
+    for cp in firsts() + sends(0, 0, 0, True):
+        cp.start()
+    for kp in range(1, p_n):
+        relay(0, kp, 0)
+    for kq in range(1, q_n):
+        relay(0, 0, kq)
+    over_a(lambda ka: relay(ka, 0, 0))
+    for kp in range(1, p_n):
+        for kq in range(1, q_n):
+            relay(0, kp, kq)
+    over_a(lambda ka: [relay(ka, kp, 0) for kp in range(1, p_n)])
+    over_a(lambda ka: [relay(ka, 0, kq) for kq in range(1, q_n)])
+    over_a(lambda ka: [relay(ka, kp, kq) for kp in range(1, p_n) for kq in range(1, q_n)])
+
+    def finish(ka):
+        for kp in range(p_n):
+            for kq in range(q_n):
+                for kc in range(1, c_n):
+                    arrived(ka, kp, kq, kc)
+                for cp in sends(ka, kp, kq):
+                    cp.wait_send()
+
+    finish(0)
+    over_a(finish)
+    for cp in firsts():
+        cp.wait_send()
     mine.wait()
 
 
@@ -158,9 +145,9 @@
         scratch_shapes=[
             dma,
             dma((a_n,)),
-            dma((a_n, b_n)),
-            dma((n_s, g_n)),
-            dma((n_s, g_n, c_n)),
+            dma((a_n, g_n)),
+            dma((a_n * g_n, b_n)),
+            dma((a_n * g_n, b_n, c_n)),
             dma((n_s, n_h)),
         ],
         compiler_params=pltpu.CompilerParams(collective_id=0, has_side_effects=True),
@@ -168,74 +155,88 @@
     )(latents)
 
 
-def attend_kernel(
-    scale, value_width, sel_ref, all_ref, q_ref, g_ref, o_ref, dq_ref, con_ref, keys, acc
-):
+def attend_kernel(scale, chunk, sel_ref, all_ref, q_ref, g_ref, o_ref, dq_ref, con_ref, keys, keys_t, acc, g_rows, o_rows):
     step = pl.program_id(0)
     block = all_ref.shape[1]
     count = sel_ref.shape[1] + 1
+    tokens, heads, value_width = g_ref.shape
+    f32, bf16 = jnp.float32, jnp.bfloat16
 
     @pl.when(step == 0)
     def _():
-        keys[:block, :] = all_ref[lax.axis_index("seq")]
-        for n in range(1, count):
-            keys[n * block : (n + 1) * block, :] = all_ref[sel_ref[0, n - 1]]
+        for n in range(count):
+            at = lax.axis_index("seq") if n == 0 else sel_ref[0, n - 1]
+            rows = all_ref[at]
+            keys[n * block : (n + 1) * block, :] = rows
+            keys_t[:, n * block : (n + 1) * block] = rows.T
         acc[...] = jnp.zeros_like(acc)
 
-    f32 = jnp.float32
-    q, g = q_ref[...], g_ref[...]
+    g_rows[...] = jnp.swapaxes(g_ref[...], 0, 1).reshape(tokens * heads, value_width)
     across = (((1,), (1,)), ((), ()))
     down = (((0,), (0,)), ((), ()))
-    scores = lax.dot_general(q, keys[...], across, preferred_element_type=f32)
-    top = jnp.max(scores, axis=-1, keepdims=True)
-    weights = jnp.exp((scores - top) * scale)
-    probs = weights * (1.0 / jnp.sum(weights, axis=-1, keepdims=True))
-    half = probs.astype(jnp.bfloat16)
     values = keys[:, :value_width]
-    out = jnp.dot(half, values, preferred_element_type=f32).astype(jnp.bfloat16)
-    o_ref[...] = out
-    delta = jnp.sum(g.astype(f32) * out.astype(f32), axis=-1, keepdims=True)
-    grad_prob = lax.dot_general(g, values, across, preferred_element_type=f32)
-    grad_score = (probs * (grad_prob - delta) * scale).astype(jnp.bfloat16)
-    dq_ref[...] = jnp.dot(grad_score, keys[...], preferred_element_type=f32).astype(jnp.bfloat16)
-    acc[...] += lax.dot_general(grad_score, q, down, preferred_element_type=f32)
-    acc[:, :value_width] += lax.dot_general(half, g, down, preferred_element_type=f32)
+    for h0 in range(0, heads, chunk):
+        hs = range(h0, h0 + chunk)
+        q = jnp.concatenate([q_ref[h] for h in hs], axis=1)
+        g = g_rows[h0 * tokens : (h0 + chunk) * tokens, :]
+        scores = jnp.dot(keys[...], q, preferred_element_type=f32)
+        top = jnp.max(scores, axis=0, keepdims=True)
+        weights = jnp.exp((scores - top) * scale)
+        probs = weights * (1.0 / jnp.sum(weights, axis=0, keepdims=True))
+        half = probs.astype(bf16)
+        grad_prob = lax.dot_general(values, g, across, preferred_element_type=f32)
+        delta = jnp.sum(half.astype(f32) * grad_prob, axis=0, keepdims=True)
+        grad_score = (probs * (grad_prob - delta) * scale).astype(bf16)
+        out = lax.dot_general(half, values, down, preferred_element_type=f32)
+        dq = jnp.dot(keys_t[...], grad_score, preferred_element_type=f32).astype(bf16)
+        for n, h in enumerate(hs):
+            dq_ref[h] = dq[:, n * tokens : (n + 1) * tokens]
+        o_rows[h0 * tokens : (h0 + chunk) * tokens, :] = out.astype(bf16)
+        acc[...] += lax.dot_general(grad_score, q, across, preferred_element_type=f32)
+        acc[:, :value_width] += jnp.dot(half, g, preferred_element_type=f32)
+    o_ref[...] = jnp.swapaxes(o_rows[...].reshape(heads, tokens, value_width), 0, 1)
 
     @pl.when(step == pl.num_programs(0) - 1)
     def _():
-        con_ref[...] = acc[...].astype(jnp.bfloat16)
+        con_ref[...] = acc[...].astype(bf16)
 
 
 def attend(selected, all_keys, queries, grad_out):
-    rows, key_width = queries.shape
-    value_width = grad_out.shape[1]
+    tokens, heads, key_width = queries.shape
+    value_width = grad_out.shape[2]
     keys = (selected.shape[1] + 1) * all_keys.shape[1]
-    tile = min(rows, 256)
-    return pl.pallas_call(
-        functools.partial(attend_kernel, key_width ** (-0.5), value_width),
-        grid=(rows // tile,),
+    group = 8 if heads % 8 == 0 else heads
+    chunk = min(4, group)
+    out, dq, con = pl.pallas_call(
+        functools.partial(attend_kernel, key_width ** (-0.5), chunk),
+        grid=(heads // group,),
         out_shape=(
-            jax.ShapeDtypeStruct((rows, value_width), jnp.bfloat16),
-            jax.ShapeDtypeStruct((rows, key_width), jnp.bfloat16),
+            jax.ShapeDtypeStruct((tokens, heads, value_width), jnp.bfloat16),
+            jax.ShapeDtypeStruct((heads, key_width, tokens), jnp.bfloat16),
             jax.ShapeDtypeStruct((keys, key_width), jnp.bfloat16),
         ),
         in_specs=[
             pl.BlockSpec(memory_space=SMEM),
             pl.BlockSpec(all_keys.shape, lambda i: (0, 0, 0)),
-            pl.BlockSpec((tile, key_width), lambda i: (i, 0)),
-            pl.BlockSpec((tile, value_width), lambda i: (i, 0)),
+            pl.BlockSpec((group, key_width, tokens), lambda i: (i, 0, 0)),
+            pl.BlockSpec((tokens, group, value_width), lambda i: (0, i, 0)),
         ],
         out_specs=(
-            pl.BlockSpec((tile, value_width), lambda i: (i, 0)),
-            pl.BlockSpec((tile, key_width), lambda i: (i, 0)),
+            pl.BlockSpec((tokens, group, value_width), lambda i: (0, i, 0)),
+            pl.BlockSpec((group, key_width, tokens), lambda i: (i, 0, 0)),
             pl.BlockSpec((keys, key_width), lambda i: (0, 0)),
         ),
         scratch_shapes=[
             pltpu.VMEM((keys, key_width), jnp.bfloat16),
+            pltpu.VMEM((key_width, keys), jnp.bfloat16),
             pltpu.VMEM((keys, key_width), jnp.float32),
+            pltpu.VMEM((tokens * group, value_width), jnp.bfloat16),
+            pltpu.VMEM((tokens * group, value_width), jnp.bfloat16),
         ],
+        compiler_params=pltpu.CompilerParams(vmem_limit_bytes=60 * 1024 * 1024),
         name="attend",
-    )(selected, all_keys, queries, grad_out)
+    )(selected, all_keys, jnp.transpose(queries, (1, 2, 0)), grad_out)
+    return out, jnp.transpose(dq, (2, 0, 1)), con
 
 
 def reduce_kernel(
@@ -387,22 +388,11 @@
 
 
 def shards(dims, queries, latents, grad_out, selected):
-    block_count, row_share, key_width = latents.shape
-    token_total, head_count, _ = queries.shape
-    value_width = grad_out.shape[2]
-    assert block_count == 1
-    rows = token_total * head_count
+    assert latents.shape[0] == 1
     pieces = gather_latents(latents, dims)
-    all_keys = pieces.reshape(pieces.shape[0], -1, key_width)
-    output, grad_query, contrib = attend(
-        selected, all_keys, queries.reshape(rows, key_width), grad_out.reshape(rows, value_width)
-    )
-    latent_grad = reduce_grads(selected, contrib, dims)
-    return (
-        output.reshape(token_total, head_count, value_width),
-        grad_query.reshape(token_total, head_count, key_width),
-        latent_grad[None],
-    )
+    all_keys = pieces.reshape(pieces.shape[0], -1, latents.shape[2])
+    output, grad_query, contrib = attend(selected, all_keys, queries, grad_out)
+    return output, grad_query, reduce_grads(selected, contrib, dims)[None]
 
 
 def solution(mesh):

time: 85.7 us -> 59.7 us (0.70)
  Pallas kernels: 73.5 us -> 57.3 us
  local copies, waits for them, and re-layouts: 11.1 us -> 1.53 us
    pallas_call x1, Pallas kernels: 32.7 us -> 21.2 us  [gather_latents(): pl.pallas_call(functools.partial(gather_kernel, dims), out_shape=jax.Shap...]
    unnamed x3 -> x1, local copies, waits for them, and re-layouts: 11.1 us -> 1.53 us
    pallas_call x1, Pallas kernels: 19.6 us -> 16.4 us  [attend(): pl.pallas_call(functools.partial(attend_kernel, key_width ** (-0.5), chun...]
    pallas_call x1, Pallas kernels: 21.3 us -> 19.7 us  [reduce_grads(): pl.pallas_call(functools.partial(reduce_kernel, dims), out_shape=jax.Shap...]
where the time goes in v2:
time: 59.7 us; the launch traced here: 59.5 us
  Pallas kernels  57.3 us (96%)
  local copies, waits for them, and re-layouts  1.53 us (3%)
  between operations  0.65 us (1%)
    pallas_call x1, Pallas kernels, gather_latents(): pl.pallas_call(functools.partial(gather_kernel, dims), out_shape=jax.Shap...  21.2 us
    pallas_call x1, Pallas kernels, reduce_grads(): pl.pallas_call(functools.partial(reduce_kernel, dims), out_shape=jax.Shap...  19.7 us
    pallas_call x1, Pallas kernels, attend(): pl.pallas_call(functools.partial(attend_kernel, key_width ** (-0.5), chun...  16.4 us
    unnamed x1, local copies, waits for them, and re-layouts  1.53 us

profile of v2, /device:TPU:0, one launch (start us, length us, event | category | flops | bytes accessed | tf_op | source)
XLA Modules:
  0.0 59.5 jit_solution(11076003932568007227)
XLA Ops:
  0.6 21.2 %gather_latents.1 = bf16[8,4,32,576]{3,2,1,0:T(8,128)(2,1)} custom-call(bf16[1,32,576]{2,1,0:T(8,128)(2,1)} %own_ref.1), custom_call_target="tpu_custom_call" | custom-call | tf_op jit(solution)/shard_map/gather_latents/pallas_call | solution.py:140
  21.9 16.4 %attend.1 = (bf16[128,16,512]{2,1,0:T(8,128)(2,1)}, bf16[16,576,128]{2,1,0:T(8,128)(2,1)}, bf16[640,576]{1,0:T(8,128)(2,1)}) custom-call(s32[1,4]{1,0:T(1,128)} %sel_ref.3, bf16[8,128,576]{2,1,0:T(8,128)(2,1)} %bitcast.5, bf16[16,576,128]{2,1,0:T(8,128)(2,1)} %bitcast.6, bf16[128,16,512]{2,1,0:T(8,128)(2,1)} %g_ref.1), custom_call_target="tpu_custom_call" | custom-call | tf_op jit(solution)/shard_map/attend/pallas_call | solution.py:210
  38.3 19.7 %reduce_grads.1 = f32[32,576]{1,0:T(8,128)} custom-call(s32[1,4]{1,0:T(1,128)} %sel_ref.3, bf16[5,2,2,32,576]{4,3,2,1,0:T(8,128)(2,1)} %bitcast.7), custom_call_target="tpu_custom_call" | custom-call | tf_op jit(solution)/shard_map/reduce_grads/pallas_call | solution.py:366
  58.0 1.5 %copy.8 = f32[1,32,576]{2,1,0:T(8,128)} copy(f32[1,32,576]{2,1,0:T(8,128)} %bitcast.8) | data formatting | bytes 147456

commit v3 on v2

--- a/solution.py
+++ b/solution.py
@@ -10,6 +10,7 @@
 MESH = pl.DeviceIdType.MESH
 VMEM = pltpu.MemorySpace.VMEM
 SMEM = pltpu.MemorySpace.SMEM
+HBM = pltpu.MemorySpace.HBM
 
 
 def place(dims):
@@ -43,12 +44,17 @@
     pl.semaphore_wait(barrier, a_n + b_n + g_n + c_n - 4)
 
 
-def gather_kernel(dims, own_ref, out_ref, own_sem, a_sem, b_sem, g_sem, c_sem, recv_sem):
+def gather_kernel(
+    dims, own_ref, g_ref, out_ref, g_out,
+    g_raw, g_in_sem, own_sem, a_sem, b_sem, g_sem, c_sem, recv_sem,
+):
     a_n, b_n, g_n, c_n = dims
     me = place(dims)
     a, b, g, c = me
     mine = pltpu.make_async_copy(own_ref.at[0], out_ref.at[a * b_n + b, g * c_n + c], own_sem)
     mine.start()
+    staged = pltpu.make_async_copy(g_ref, g_raw, g_in_sem)
+    staged.start()
     greet(dims, me)
 
     swap = b_n == g_n
@@ -105,6 +111,8 @@
 
     for cp in firsts() + sends(0, 0, 0, True):
         cp.start()
+    staged.wait()
+    g_out[...] = jnp.swapaxes(g_raw[...], 0, 1)
     for kp in range(1, p_n):
         relay(0, kp, 0)
     for kq in range(1, q_n):
@@ -132,17 +140,23 @@
     mine.wait()
 
 
-def gather_latents(latents, dims):
+def gather_latents(latents, grad_out, dims):
     a_n, b_n, g_n, c_n = dims
     _, row_share, key_width = latents.shape
     n_s, n_h = a_n * b_n, g_n * c_n
+    tokens, heads, value_width = grad_out.shape
     dma = pltpu.SemaphoreType.DMA
     return pl.pallas_call(
         functools.partial(gather_kernel, dims),
-        out_shape=jax.ShapeDtypeStruct((n_s, n_h, row_share, key_width), latents.dtype),
-        in_specs=[pl.BlockSpec(memory_space=VMEM)],
-        out_specs=pl.BlockSpec(memory_space=VMEM),
+        out_shape=(
+            jax.ShapeDtypeStruct((n_s, n_h, row_share, key_width), latents.dtype),
+            jax.ShapeDtypeStruct((heads, tokens, value_width), grad_out.dtype),
+        ),
+        in_specs=[pl.BlockSpec(memory_space=HBM)] * 2,
+        out_specs=[pl.BlockSpec(memory_space=VMEM)] * 2,
         scratch_shapes=[
+            pltpu.VMEM(grad_out.shape, grad_out.dtype),
+            dma,
             dma,
             dma((a_n,)),
             dma((a_n, g_n)),
@@ -150,16 +164,16 @@
             dma((a_n * g_n, b_n, c_n)),
             dma((n_s, n_h)),
         ],
-        compiler_params=pltpu.CompilerParams(collective_id=0, has_side_effects=True),
+        compiler_params=pltpu.CompilerParams(collective_id=0, has_side_effects=True, vmem_limit_bytes=67043328 - 14000000),
         name="gather_latents",
-    )(latents)
-
-
-def attend_kernel(scale, chunk, sel_ref, all_ref, q_ref, g_ref, o_ref, dq_ref, con_ref, keys, keys_t, acc, g_rows, o_rows):
+    )(latents, grad_out)
+
+
+def attend_kernel(scale, chunk, sel_ref, all_ref, q_ref, g_ref, o_ref, dq_ref, con_ref, keys, keys_t, acc, o_rows):
     step = pl.program_id(0)
     block = all_ref.shape[1]
     count = sel_ref.shape[1] + 1
-    tokens, heads, value_width = g_ref.shape
+    heads, tokens, value_width = g_ref.shape
     f32, bf16 = jnp.float32, jnp.bfloat16
 
     @pl.when(step == 0)
@@ -171,14 +185,13 @@
             keys_t[:, n * block : (n + 1) * block] = rows.T
         acc[...] = jnp.zeros_like(acc)
 
-    g_rows[...] = jnp.swapaxes(g_ref[...], 0, 1).reshape(tokens * heads, value_width)
     across = (((1,), (1,)), ((), ()))
     down = (((0,), (0,)), ((), ()))
     values = keys[:, :value_width]
     for h0 in range(0, heads, chunk):
         hs = range(h0, h0 + chunk)
         q = jnp.concatenate([q_ref[h] for h in hs], axis=1)
-        g = g_rows[h0 * tokens : (h0 + chunk) * tokens, :]
+        g = g_ref[h0 : h0 + chunk].reshape(chunk * tokens, value_width)
         scores = jnp.dot(keys[...], q, preferred_element_type=f32)
         top = jnp.max(scores, axis=0, keepdims=True)
         weights = jnp.exp((scores - top) * scale)
@@ -202,7 +215,7 @@
 
 
 def attend(selected, all_keys, queries, grad_out):
-    tokens, heads, key_width = queries.shape
+    heads, key_width, tokens = queries.shape
     value_width = grad_out.shape[2]
     keys = (selected.shape[1] + 1) * all_keys.shape[1]
     group = 8 if heads % 8 == 0 else heads
@@ -219,7 +232,7 @@
             pl.BlockSpec(memory_space=SMEM),
             pl.BlockSpec(all_keys.shape, lambda i: (0, 0, 0)),
             pl.BlockSpec((group, key_width, tokens), lambda i: (i, 0, 0)),
-            pl.BlockSpec((tokens, group, value_width), lambda i: (0, i, 0)),
+            pl.BlockSpec((group, tokens, value_width), lambda i: (i, 0, 0)),
         ],
         out_specs=(
             pl.BlockSpec((tokens, group, value_width), lambda i: (0, i, 0)),
@@ -231,11 +244,10 @@
             pltpu.VMEM((key_width, keys), jnp.bfloat16),
             pltpu.VMEM((keys, key_width), jnp.float32),
             pltpu.VMEM((tokens * group, value_width), jnp.bfloat16),
-            pltpu.VMEM((tokens * group, value_width), jnp.bfloat16),
         ],
-        compiler_params=pltpu.CompilerParams(vmem_limit_bytes=60 * 1024 * 1024),
+        compiler_params=pltpu.CompilerParams(vmem_limit_bytes=67043328 - 16000000),
         name="attend",
-    )(selected, all_keys, jnp.transpose(queries, (1, 2, 0)), grad_out)
+    )(selected, all_keys, queries, grad_out)
     return out, jnp.transpose(dq, (2, 0, 1)), con
 
 
@@ -275,7 +287,8 @@
     def to_a(k):
         return copy(a_out.at[k], a_in.at[k], a_sem.at[k], (other(a, k, a_n), b, g, c))
 
-    for p in range(count):
+    order = list(range(1, count)) + [0]
+    for p in order:
         for k in range(1, c_n):
             to_c(p, k).start()
 
@@ -285,23 +298,27 @@
             total += c_in[p, k, g1].astype(f32)
         return total
 
-    for p in range(count):
+    for p in order:
         for k in range(1, c_n):
             to_c(p, k).wait_recv()
         for k in range(1, g_n):
             g_out[p, k] = chip_sum(p, other(g, k, g_n)).astype(bf16)
             to_g(p, k).start()
-    sums[count] = jnp.zeros(sums.shape[1:], f32)
-    for p in range(count):
+
+    def head_sum(p):
         total = chip_sum(p, g)
         for k in range(1, g_n):
             to_g(p, k).wait_recv()
             total += g_in[p, k].astype(f32)
-        sums[p] = total
+        return total
+
+    sums[0] = jnp.zeros(sums.shape[1:], f32)
+    for p in range(1, count):
+        sums[p] = head_sum(p)
 
     def dense(a1, b1):
         block = a1 * b_n + b1
-        at = jnp.where(block == a * b_n + b, 0, count)
+        at = 0
         for n in range(1, count):
             at = jnp.where(sel_ref[0, n - 1] == block, n, at)
         return sums[at]
@@ -325,7 +342,7 @@
         lax.fori_loop(1, a_n, send_b, 0)
         send_b(0, 0)
     lax.fori_loop(1, a_n, send_a, 0)
-    total = dense(a, b)
+    total = head_sum(0)
     for n in range(1, b_n):
         to_b(0, n).wait_recv()
         total += b_in[0, n].astype(f32)
@@ -372,7 +389,7 @@
             half((count, c_n, g_n) + one),
             half((count, g_n) + one),
             half((count, g_n) + one),
-            pltpu.VMEM((count + 1,) + one, jnp.float32),
+            pltpu.VMEM((count,) + one, jnp.float32),
             half((a_n, b_n) + one),
             half((a_n, b_n) + one),
             half((a_n,) + one),
@@ -382,16 +399,18 @@
             dma((a_n, b_n, 2)),
             dma((a_n, 2)),
         ],
-        compiler_params=pltpu.CompilerParams(collective_id=1, has_side_effects=True),
+        compiler_params=pltpu.CompilerParams(collective_id=1, has_side_effects=True, vmem_limit_bytes=12 * 1024 * 1024),
         name="reduce_grads",
     )(selected, contrib)
 
 
 def shards(dims, queries, latents, grad_out, selected):
     assert latents.shape[0] == 1
-    pieces = gather_latents(latents, dims)
+    pieces, grad_out = gather_latents(latents, grad_out, dims)
     all_keys = pieces.reshape(pieces.shape[0], -1, latents.shape[2])
-    output, grad_query, contrib = attend(selected, all_keys, queries, grad_out)
+    output, grad_query, contrib = attend(
+        selected, all_keys, jnp.transpose(queries, (1, 2, 0)), grad_out
+    )
     return output, grad_query, reduce_grads(selected, contrib, dims)[None]
 
 

time: 59.7 us -> 54.6 us (0.915)
  Pallas kernels: 57.3 us -> 52.3 us
    pallas_call x1, Pallas kernels: 19.7 us -> 17.6 us  [reduce_grads(): pl.pallas_call(functools.partial(reduce_kernel, dims), out_shape=jax.Shap...]
    pallas_call x1, Pallas kernels: 21.2 us -> 19.4 us  [gather_latents(): pl.pallas_call(functools.partial(gather_kernel, dims), out_shape=(jax.Sha...]
    pallas_call x1, Pallas kernels: 16.4 us -> 15.3 us  [attend(): pl.pallas_call(functools.partial(attend_kernel, key_width ** (-0.5), chun...]
    unnamed x1 -> x5, local copies, waits for them, and re-layouts: 1.53 us -> 1.42 us
where the time goes in v3:
time: 54.6 us; the launch traced here: 54.4 us
  Pallas kernels  52.3 us (96%)
  local copies, waits for them, and re-layouts  1.42 us (3%)
  between operations  0.67 us (1%)
    pallas_call x1, Pallas kernels, gather_latents(): pl.pallas_call(functools.partial(gather_kernel, dims), out_shape=(jax.Sha...  19.4 us
    pallas_call x1, Pallas kernels, reduce_grads(): pl.pallas_call(functools.partial(reduce_kernel, dims), out_shape=jax.Shap...  17.6 us
    pallas_call x1, Pallas kernels, attend(): pl.pallas_call(functools.partial(attend_kernel, key_width ** (-0.5), chun...  15.3 us
    unnamed x5, local copies, waits for them, and re-layouts  1.42 us

profile of v3, /device:TPU:0, one launch (start us, length us, event | category | flops | bytes accessed | tf_op | source)
XLA Modules:
  0.0 54.4 jit_solution(15197205165592000570)
XLA Ops:
  0.6 0.0 copy-start.1
  0.6 0.0 copy-start
  0.7 0.8 %copy-done = bf16[1,32,576]{2,1,0:T(8,128)(2,1)S(1)} copy-done((bf16[1,32,576]{2,1,0:T(8,128)(2,1)S(1)}, bf16[1,32,576]{2,1,0:T(8,128)(2,1)}, u32[]{:S(2)}) %copy-start) | copy-done | bytes 36888
  1.4 19.4 %gather_latents.1 = (bf16[8,4,32,576]{3,2,1,0:T(8,128)(2,1)S(1)}, bf16[16,128,512]{2,1,0:T(8,128)(2,1)S(1)}) custom-call(bf16[1,32,576]{2,1,0:T(8,128)(2,1)S(1)} %copy-done, bf16[128,16,512]{2,1,0:T(8,128)(2,1)} %g_ref.1), custom_call_target="tpu_custom_call" | custom-call | tf_op jit(solution)/shard_map/gather_latents/pallas_call | solution.py:149
  20.8 0.0 copy-done.1
  20.8 15.3 %attend.1 = (bf16[128,16,512]{2,1,0:T(8,128)(2,1)}, bf16[16,576,128]{2,1,0:T(8,128)(2,1)}, bf16[640,576]{1,0:T(8,128)(2,1)S(1)}) custom-call(s32[1,4]{1,0:T(1,128)S(1)} %copy-done.1, bf16[8,128,576]{2,1,0:T(8,128)(2,1)S(1)} %bitcast.5, bf16[16,576,128]{2,1,0:T(8,128)(2,1)} %bitcast.8, bf16[16,128,512]{2,1,0:T(8,128)(2,1)S(1)} %get-tuple-element.9.g_ref), custom_call_target="tpu_custom_call" | custom-call | tf_op jit(solution)/shard_map/attend/pallas_call | solution.py:223
  36.2 17.6 %reduce_grads.1 = f32[32,576]{1,0:T(8,128)S(1)} custom-call(s32[1,4]{1,0:T(1,128)S(1)} %copy-done.1, bf16[5,2,2,32,576]{4,3,2,1,0:T(8,128)(2,1)S(1)} %bitcast.6), custom_call_target="tpu_custom_call" | custom-call | tf_op jit(solution)/shard_map/reduce_grads/pallas_call | solution.py:383
  53.8 0.6 %copy.8 = f32[1,32,576]{2,1,0:T(8,128)} copy(f32[1,32,576]{2,1,0:T(8,128)S(1)} %bitcast.7) | data formatting | bytes 147456
Async XLA Ops:
  0.6 20.2 %copy-start.1 = (s32[1,4]{1,0:T(1,128)S(1)}, s32[1,4]{1,0:T(1,128)}, u32[]{:S(2)}) copy-start(s32[1,4]{1,0:T(1,128)} %sel_ref.3) | copy-start | bytes 52
  0.6 0.8 %copy-start = (bf16[1,32,576]{2,1,0:T(8,128)(2,1)S(1)}, bf16[1,32,576]{2,1,0:T(8,128)(2,1)}, u32[]{:S(2)}) copy-start(bf16[1,32,576]{2,1,0:T(8,128)(2,1)} %own_ref.1) | copy-start | bytes 110596

commit v4 on v3

--- a/solution.py
+++ b/solution.py
@@ -219,7 +219,7 @@
     value_width = grad_out.shape[2]
     keys = (selected.shape[1] + 1) * all_keys.shape[1]
     group = 8 if heads % 8 == 0 else heads
-    chunk = min(4, group)
+    chunk = min(8, group)
     out, dq, con = pl.pallas_call(
         functools.partial(attend_kernel, key_width ** (-0.5), chunk),
         grid=(heads // group,),

time: 54.6 us -> 54.7 us (level)
  no operation moved by 1% of the time
where the time goes in v4:
time: 54.7 us; the launch traced here: 54.5 us
  Pallas kernels  52.4 us (96%)
  local copies, waits for them, and re-layouts  1.42 us (3%)
  between operations  0.67 us (1%)
    pallas_call x1, Pallas kernels, gather_latents(): pl.pallas_call(functools.partial(gather_kernel, dims), out_shape=(jax.Sha...  19.4 us
    pallas_call x1, Pallas kernels, reduce_grads(): pl.pallas_call(functools.partial(reduce_kernel, dims), out_shape=jax.Shap...  17.6 us
    pallas_call x1, Pallas kernels, attend(): pl.pallas_call(functools.partial(attend_kernel, key_width ** (-0.5), chun...  15.4 us
    unnamed x5, local copies, waits for them, and re-layouts  1.42 us

profile of v4, /device:TPU:0, one launch (start us, length us, event | category | flops | bytes accessed | tf_op | source)
XLA Modules:
  0.0 54.5 jit_solution(11706058564769271143)
XLA Ops:
  0.6 0.0 copy-start.1
  0.6 0.0 copy-start
  0.7 0.8 %copy-done = bf16[1,32,576]{2,1,0:T(8,128)(2,1)S(1)} copy-done((bf16[1,32,576]{2,1,0:T(8,128)(2,1)S(1)}, bf16[1,32,576]{2,1,0:T(8,128)(2,1)}, u32[]{:S(2)}) %copy-start) | copy-done | bytes 36888
  1.4 19.4 %gather_latents.1 = (bf16[8,4,32,576]{3,2,1,0:T(8,128)(2,1)S(1)}, bf16[16,128,512]{2,1,0:T(8,128)(2,1)S(1)}) custom-call(bf16[1,32,576]{2,1,0:T(8,128)(2,1)S(1)} %copy-done, bf16[128,16,512]{2,1,0:T(8,128)(2,1)} %g_ref.1), custom_call_target="tpu_custom_call" | custom-call | tf_op jit(solution)/shard_map/gather_latents/pallas_call | solution.py:149
  20.8 0.0 copy-done.1
  20.8 15.4 %attend.1 = (bf16[128,16,512]{2,1,0:T(8,128)(2,1)}, bf16[16,576,128]{2,1,0:T(8,128)(2,1)}, bf16[640,576]{1,0:T(8,128)(2,1)S(1)}) custom-call(s32[1,4]{1,0:T(1,128)S(1)} %copy-done.1, bf16[8,128,576]{2,1,0:T(8,128)(2,1)S(1)} %bitcast.5, bf16[16,576,128]{2,1,0:T(8,128)(2,1)} %bitcast.8, bf16[16,128,512]{2,1,0:T(8,128)(2,1)S(1)} %get-tuple-element.9.g_ref), custom_call_target="tpu_custom_call" | custom-call | tf_op jit(solution)/shard_map/attend/pallas_call | solution.py:223
  36.2 17.6 %reduce_grads.1 = f32[32,576]{1,0:T(8,128)S(1)} custom-call(s32[1,4]{1,0:T(1,128)S(1)} %copy-done.1, bf16[5,2,2,32,576]{4,3,2,1,0:T(8,128)(2,1)S(1)} %bitcast.6), custom_call_target="tpu_custom_call" | custom-call | tf_op jit(solution)/shard_map/reduce_grads/pallas_call | solution.py:383
  53.9 0.6 %copy.8 = f32[1,32,576]{2,1,0:T(8,128)} copy(f32[1,32,576]{2,1,0:T(8,128)S(1)} %bitcast.7) | data formatting | bytes 147456
Async XLA Ops:
  0.6 20.2 %copy-start.1 = (s32[1,4]{1,0:T(1,128)S(1)}, s32[1,4]{1,0:T(1,128)}, u32[]{:S(2)}) copy-start(s32[1,4]{1,0:T(1,128)} %sel_ref.3) | copy-start | bytes 52
  0.6 0.8 %copy-start = (bf16[1,32,576]{2,1,0:T(8,128)(2,1)S(1)}, bf16[1,32,576]{2,1,0:T(8,128)(2,1)}, u32[]{:S(2)}) copy-start(bf16[1,32,576]{2,1,0:T(8,128)(2,1)} %own_ref.1) | copy-start | bytes 110596
